TPU v7x, 32 devices: a whole 2x2x4 slice. The times are simulated.
32 devices in a mesh: rows: 8 (over z, core), pairs: 4 (over y, x).
Axes of the slice: x: 2, y: 2, z: 4, core: 2. Of those that a mesh axis runs over, the one named last changes fastest.
Arguments:
- observed: float32 [12288, 2048], P('rows', 'pairs'), as said below
- estimate: float32 [12288, 2048], P('rows', 'pairs'), may hold values from -0.054126587 to 0.054126587
- mask: int32 [12288, 2048], P('rows', 'pairs'), may hold values from 0 to 1
- threshold: float32 [2048], P('pairs'), may hold values from 0.02 to 0.12
Outputs:
- regrouped: float32 [2048, 12288], P(('rows', 'pairs'))
Inputs may be any that keep to these rules, and one draw needn't show every extreme that they name: observed has entries of order 12288^-1/2.
All inputs are finite; a program needn't handle non-finite values.
Results may differ from a plain program's by a relative error of at most 0.0003.
Values sent between devices are 32-bit elements; how exact they have to be, the bound alone decides.
A program may use at most 128 MiB of HBM per device.

v0:
```python
import jax
import jax.numpy as jnp
from jax import lax
from jax.sharding import PartitionSpec as P

ROUNDS = 4
NS_STEPS = 3


HI = lax.Precision.HIGHEST


def from_behind(block, axis, distance):
    devices = range(lax.axis_size(axis))
    route = [((i - distance) % len(devices), i) for i in devices]
    return lax.ppermute(block, axis, route)


def whitening_of(gram):
    width = gram.shape[-1]
    eye = jnp.eye(width, dtype=jnp.float32)
    dsum = jnp.diagonal(gram, axis1=-2, axis2=-1) + 1e-06
    inv_root = 1.0 / jnp.sqrt(dsum)
    normed = gram * inv_root[..., :, None] * inv_root[..., None, :]
    fro = jnp.sqrt(jnp.sum(normed * normed, axis=(-2, -1)))
    ymat = normed / fro[..., None, None]
    zmat = jnp.broadcast_to(eye, normed.shape)
    for step in range(NS_STEPS):
        tmat = 1.5 * eye - 0.5 * jnp.einsum("pij,pjk->pik", zmat, ymat, precision=HI)
        ymat = jnp.einsum("pij,pjk->pik", ymat, tmat, precision=HI)
        zmat = jnp.einsum("pij,pjk->pik", tmat, zmat, precision=HI)
    return (
        inv_root[..., :, None]
        * zmat
        * jnp.sqrt(dsum)[..., None, :]
        / jnp.sqrt(fro)[..., None, None]
    )


def on_device(observed, estimate, mask, threshold):
    filled = jnp.where(mask == 1, observed, estimate)
    rows_here, width = filled.shape
    block = width // 4
    for round_index in range(ROUNDS):
        pairs = filled.reshape(rows_here, 2, 2 * block)
        partial_gram = jnp.einsum("rpi,rpj->pij", pairs, pairs, precision=HI)
        gram = lax.psum(partial_gram, "rows")
        whitening = whitening_of(gram)
        pairs = jnp.einsum("rpi,pij->rpj", pairs, whitening, precision=HI)
        quads = pairs.reshape(rows_here, 4, block)
        if round_index + 1 < ROUNDS:
            moved = from_behind(quads[:, 3], "pairs", 1)
            quads = jnp.stack([quads[:, 0], moved, quads[:, 2], quads[:, 1]], axis=1)
        filled = quads.reshape(rows_here, width)
    squares = lax.psum(jnp.sum(filled * filled, axis=0), "rows")
    col_norm = jnp.sqrt(squares + 1e-06)
    factor = jnp.maximum(col_norm - threshold, 0.0) / col_norm
    shrunk_t = (filled * factor[None, :]).T
    count_rows = lax.axis_size("rows")
    count_pairs = lax.axis_size("pairs")
    each_dest = width // (count_rows * count_pairs)
    packed = shrunk_t.reshape(count_rows * count_pairs, each_dest, rows_here)
    landed = lax.all_to_all(packed, ("rows", "pairs"), split_axis=0, concat_axis=1, tiled=True)
    landed = landed.reshape(count_rows, count_pairs, each_dest, rows_here).transpose(2, 1, 0, 3)
    return landed.reshape(each_dest * count_pairs, count_rows * rows_here)


def solution(mesh):
    placed = (P("rows", "pairs"), P("rows", "pairs"), P("rows", "pairs"), P("pairs"))
    return jax.shard_map(
        on_device, mesh=mesh, in_specs=placed, out_specs=P(("rows", "pairs"), None), check_vma=False
    )
```

profile of v0, /device:TPU:0, one launch (start us, length us, event | category | flops | bytes accessed | tf_op | source)
XLA Modules:
  0.0 571.2 jit_solution(13144928827066859881)
XLA Ops:
  6.5 4.9 compare_select_fusion
  11.4 6.2 %fusion.2 = f32[2,256,256]{2,1,0:T(8,128)} fusion(f32[192,2,8,256]{3,2,1,0:T(8,128)S(1)} %bitcast.133), kind=kOutput, calls=%fused_computation.6 | convolution fusion | flops 2415919104 | bytes 3670016 | tf_op jit(solution)/shard_map/rpi,rpj->pij/dot_general | solution.py:46
  18.5 58.6 %all-reduce.5.cloned.1.call-done = f32[2,256,256]{2,1,0:T(8,128)} async-done(((f32[2,256,256]{2,1,0:T(8,128)}), f32[2,256,256]{2,1,0:T(8,128)}) %all-reduce.5.cloned.1.call-update) | async-done | bytes 524304 | tf_op jit(solution)/shard_map/psum | solution.py:47
  77.0 17.5 %copy.62 = f32[2,256,256]{0,2,1:T(8,128)} copy(f32[2,256,256]{2,1,0:T(8,128)} %all-reduce.5.cloned.1.call-done) | data formatting | bytes 1048576 | tf_op jit(solution)/shard_map/psum | solution.py:47
  94.5 3.0 gather_fusion
  97.5 1.6 sqrt_bitcast_fusion.3
  99.1 1.0 copy.63
  100.1 1.4 multiply_reduce_fusion.3
  101.5 1.9 fusion.26
  105.4 1.4 fusion.60
  106.8 1.4 fusion.61
  108.4 1.9 fusion.24
  110.2 1.7 fusion.23
  112.0 5.3 fusion
  117.6 1.5 collective-permute-start
  119.1 16.9 %collective-permute-done = f32[1536,128]{0,1:T(8,128)S(1)} collective-permute-done((f32[1536,128]{0,1:T(8,128)S(1)}, f32[1536,128]{0,1:T(8,128)S(1)}, u32[]{:S(2)}, u32[]{:S(2)}) %collective-permute-start) | collective-permute-done | bytes 786464 | tf_op jit(solution)/shard_map/ppermute | solution.py:16
  136.4 3.9 fusion.62
  140.8 55.3 %all-reduce.7.cloned.1.call-done = f32[2,256,256]{2,1,0:T(8,128)} async-done(((f32[2,256,256]{2,1,0:T(8,128)}), f32[2,256,256]{2,1,0:T(8,128)}) %all-reduce.7.cloned.1.call-update) | async-done | bytes 524304 | tf_op jit(solution)/shard_map/psum | solution.py:47
  196.0 17.3 %copy.69 = f32[2,256,256]{0,2,1:T(8,128)} copy(f32[2,256,256]{2,1,0:T(8,128)} %all-reduce.7.cloned.1.call-done) | data formatting | bytes 1048576 | tf_op jit(solution)/shard_map/psum | solution.py:47
  213.3 3.0 gather_fusion.1
  216.3 1.6 sqrt_bitcast_fusion.2
  217.9 1.0 copy.70
  218.8 1.4 multiply_reduce_fusion.2
  220.2 1.9 fusion.21
  224.2 1.5 fusion.63
  225.6 1.4 fusion.64
  227.1 1.9 fusion.19
  229.0 1.7 fusion.18
  230.7 3.1 fusion.65
  234.1 1.7 collective-permute-start.1
  235.8 16.9 %collective-permute-done.1 = f32[1536,128]{0,1:T(8,128)S(1)} collective-permute-done((f32[1536,128]{0,1:T(8,128)S(1)}, f32[1536,128]{0,1:T(8,128)S(1)}, u32[]{:S(2)}, u32[]{:S(2)}) %collective-permute-start.1) | collective-permute-done | bytes 786464 | tf_op jit(solution)/shard_map/ppermute | solution.py:16
  253.0 3.9 fusion.66
  257.0 55.7 %all-reduce.9.cloned.1.call-done = f32[2,256,256]{2,1,0:T(8,128)} async-done(((f32[2,256,256]{2,1,0:T(8,128)}), f32[2,256,256]{2,1,0:T(8,128)}) %all-reduce.9.cloned.1.call-update) | async-done | bytes 524304 | tf_op jit(solution)/shard_map/psum | solution.py:47
  312.6 17.3 %copy.76 = f32[2,256,256]{0,2,1:T(8,128)} copy(f32[2,256,256]{2,1,0:T(8,128)} %all-reduce.9.cloned.1.call-done) | data formatting | bytes 1048576 | tf_op jit(solution)/shard_map/psum | solution.py:47
  329.9 3.0 gather_fusion.2
  332.9 1.6 sqrt_bitcast_fusion.1
  334.5 1.0 copy.77
  335.5 1.4 multiply_reduce_fusion.1
  336.9 1.9 fusion.16
  340.8 1.4 fusion.67
  342.2 1.4 fusion.68
  343.8 1.9 fusion.14
  345.6 1.7 fusion.13
  347.4 3.1 fusion.69
  350.7 1.7 collective-permute-start.2
  352.5 16.9 %collective-permute-done.2 = f32[1536,128]{0,1:T(8,128)S(1)} collective-permute-done((f32[1536,128]{0,1:T(8,128)S(1)}, f32[1536,128]{0,1:T(8,128)S(1)}, u32[]{:S(2)}, u32[]{:S(2)}) %collective-permute-start.2) | collective-permute-done | bytes 786464 | tf_op jit(solution)/shard_map/ppermute | solution.py:16
  369.7 3.9 fusion.70
  373.6 55.7 %all-reduce.11.cloned.1.call-done = f32[2,256,256]{2,1,0:T(8,128)} async-done(((f32[2,256,256]{2,1,0:T(8,128)}), f32[2,256,256]{2,1,0:T(8,128)}) %all-reduce.11.cloned.1.call-update) | async-done | bytes 524304 | tf_op jit(solution)/shard_map/psum | solution.py:47
  429.3 17.3 %copy.83 = f32[2,256,256]{0,2,1:T(8,128)} copy(f32[2,256,256]{2,1,0:T(8,128)} %all-reduce.11.cloned.1.call-done) | data formatting | bytes 1048576 | tf_op jit(solution)/shard_map/psum | solution.py:47
  446.6 3.0 gather_fusion.3
  449.6 1.6 sqrt_bitcast_fusion
  451.2 1.0 copy.84
  452.1 1.4 multiply_reduce_fusion
  453.5 1.9 fusion.11
  457.5 1.5 fusion.71
  458.9 1.4 fusion.72
  460.4 1.9 fusion.9
  462.3 1.7 fusion.8
  464.1 4.7 fusion.4
  468.8 13.7 %psum.39 = f32[512]{0:T(512)S(1)} all-reduce(f32[512]{0:T(512)S(1)} %bitcast.145), channel_id=1, replica_groups=mesh['rows'=8,'pairs'=4] {'rows'}, use_global_device_ids=true, to_apply=%region_9.10 | all-reduce | flops 512 | bytes 4096 | tf_op jit(solution)/shard_map/psum | solution.py:55
  482.5 2.2 bitcast_multiply_fusion
  484.7 74.3 %all_to_all.4 = f32[32,16,1536]{2,1,0:T(8,128)S(1)} all-to-all(f32[32,16,1536]{2,1,0:T(8,128)S(1)} %bitcast.135), channel_id=1, replica_groups=mesh['rows'=8,'pairs'=4] {'rows','pairs'}, dimensions={0} | all-to-all | bytes 6291456 | tf_op jit(solution)/shard_map/all_to_all | solution.py:63
  559.0 1.8 copy.89
  560.8 3.4 copy.102
  (57 shorter events, 11.5 us)
Async XLA Ops:
  6.5 70.5 %all-reduce.5.cloned.1.call-start = ((), (), s32[]{:S(2)}) async-start(), calls=%async_computation.1 | async-start | bytes 1048576 | tf_op jit(solution)/shard_map/psum | solution.py:47
  17.7 178.4 %all-reduce.7.cloned.1.call-start = ((), (), s32[]{:S(2)}) async-start(), calls=%async_computation.2 | async-start | bytes 1048576 | tf_op jit(solution)/shard_map/psum | solution.py:47
  100.1 3.3 copy-start
  100.1 3.9 copy-start.4
  117.6 18.5 %collective-permute-start = (f32[1536,128]{0,1:T(8,128)S(1)}, f32[1536,128]{0,1:T(8,128)S(1)}, u32[]{:S(2)}, u32[]{:S(2)}) collective-permute-start(f32[1536,128]{0,1:T(8,128)S(1)} %get-tuple-element.16), channel_id=1, source_target_pairs={{3,0},{0,1},{1,2},{2,3},{7,4},{4,5},{5,6},{6,7},{11,8},{8,9},{9,10... | collective-permute-start | bytes 2359304 | tf_op jit(solution)/shard_map/ppermute | solution.py:16
  140.2 172.4 %all-reduce.9.cloned.1.call-start = ((), (), s32[]{:S(2)}) async-start(), calls=%async_computation.3 | async-start | bytes 1048576 | tf_op jit(solution)/shard_map/psum | solution.py:47
  218.8 3.3 copy-start.1
  218.8 3.9 copy-start.5
  234.1 18.6 %collective-permute-start.1 = (f32[1536,128]{0,1:T(8,128)S(1)}, f32[1536,128]{0,1:T(8,128)S(1)}, u32[]{:S(2)}, u32[]{:S(2)}) collective-permute-start(f32[1536,128]{0,1:T(8,128)S(1)} %get-tuple-element.12), channel_id=1, source_target_pairs={{3,0},{0,1},{1,2},{2,3},{7,4},{4,5},{5,6},{6,7},{11,8},{8,9},{9,10... | collective-permute-start | bytes 2359304 | tf_op jit(solution)/shard_map/ppermute | solution.py:16
  256.9 172.4 %all-reduce.11.cloned.1.call-start = ((), (), s32[]{:S(2)}) async-start(), calls=%async_computation.4 | async-start | bytes 1048576 | tf_op jit(solution)/shard_map/psum | solution.py:47
  335.5 3.3 copy-start.2
  335.5 3.9 copy-start.6
  350.7 18.7 %collective-permute-start.2 = (f32[1536,128]{0,1:T(8,128)S(1)}, f32[1536,128]{0,1:T(8,128)S(1)}, u32[]{:S(2)}, u32[]{:S(2)}) collective-permute-start(f32[1536,128]{0,1:T(8,128)S(1)} %get-tuple-element.8), channel_id=1, source_target_pairs={{3,0},{0,1},{1,2},{2,3},{7,4},{4,5},{5,6},{6,7},{11,8},{8,9},{9,10... | collective-permute-start | bytes 2359304 | tf_op jit(solution)/shard_map/ppermute | solution.py:16
  452.1 3.3 copy-start.3
  452.1 3.9 copy-start.7
  464.0 18.4 %copy-start.8 = (f32[512]{0:T(512)S(1)}, f32[512]{0:T(512)}, u32[]{:S(2)}) copy-start(f32[512]{0:T(512)} %param.7) | copy-start | bytes 6148
Sparse Core Ops, SparseCore 0:
  17.8 59.2 all-reduce.4
  140.4 55.6 all-reduce.6
  257.0 55.5 all-reduce.8
  373.7 55.5 all-reduce.10
where the time goes:
time: 579 us; the launch traced here: 571 us
  waiting for transfers between devices  276 us (48%)
  local copies, waits for them, and re-layouts  91.6 us (16%)
  blocking collectives  88 us (15%)
  matrix products  75.5 us (13%)
  other arithmetic  20.6 us (4%)
  between operations  14 us (2%)
    psum x4, waiting for transfers between devices, on_device(): gram = lax.psum(partial_gram, 'rows')  225 us
    all_to_all x1, blocking collectives, on_device(): lax.all_to_all(packed, ('rows', 'pairs'), split_axis=0, concat_axis=1, ti...  74.3 us
    psum x4, local copies, waits for them, and re-layouts, on_device(): gram = lax.psum(partial_gram, 'rows')  69.3 us
    ppermute x3, waiting for transfers between devices, from_behind(): return lax.ppermute(block, axis, route)  50.8 us
    dot_general x4, matrix products, on_device(): partial_gram = jnp.einsum('rpi,rpj->pij', pairs, pairs, precision=HI)  17.7 us
    dot_general x12, matrix products, whitening_of(): jnp.einsum('pij,pjk->pik', zmat, ymat, precision=HI)  17.6 us
    dot_general x4, matrix products, on_device(): pairs = jnp.einsum('rpi,pij->rpj', pairs, whitening, precision=HI)  16.3 us
    dot_general x12, matrix products, whitening_of(): zmat = jnp.einsum('pij,pjk->pik', tmat, zmat, precision=HI)  15.2 us
  transfers between devices with their start and end apart: 7, of which 7 were waited for; matrix products, arithmetic and copies ran while one was open for 0% of the time, Pallas kernels for 0%

commit v1 on v0

v1 whole, which is shorter than its diff:
```python
import functools

import jax
import jax.numpy as jnp
from jax import lax
from jax.experimental import pallas as pl
from jax.experimental.pallas import tpu as pltpu
from jax.sharding import PartitionSpec as P

MESH = pl.DeviceIdType.MESH
F32 = jnp.float32
BF16 = jnp.bfloat16
NN = (((1,), (0,)), ((), ()))
NT = (((1,), (1,)), ((), ()))


def split(a):
    high = a.astype(BF16)
    return high, (a - high.astype(F32)).astype(BF16)


def dot_parts(a, b, dims):
    def one(x, y):
        return lax.dot_general(x, y, dims, preferred_element_type=F32)

    return one(a[0], b[0]) + (one(a[0], b[1]) + one(a[1], b[0]))


def dot3(a, b, dims=NN):
    return dot_parts(split(a), split(b), dims)


def whitening_t(gram):
    width = gram.shape[0]
    eye = (
        lax.broadcasted_iota(jnp.int32, (width, width), 0)
        == lax.broadcasted_iota(jnp.int32, (width, width), 1)
    ).astype(F32)
    on_diag = gram * eye
    d_col = jnp.sum(on_diag, axis=1, keepdims=True) + 1e-06
    d_row = jnp.sum(on_diag, axis=0, keepdims=True) + 1e-06
    i_col = 1.0 / jnp.sqrt(d_col)
    i_row = 1.0 / jnp.sqrt(d_row)
    normed = gram * i_col * i_row
    sq = jnp.sum(jnp.sum(normed * normed, axis=1, keepdims=True), axis=0, keepdims=True)
    fro = jnp.sqrt(sq)
    y = normed / fro
    t = 1.5 * eye - 0.5 * y
    z = t
    y = dot3(y, t)
    t = 1.5 * eye - 0.5 * dot3(z, y)
    y, z = dot3(y, t), dot3(t, z)
    t = 1.5 * eye - 0.5 * dot3(z, y)
    z = dot3(t, z)
    return jnp.sqrt(d_col) * z * i_row / jnp.sqrt(fro)


def join(ss, sm, mm):
    top = jnp.concatenate([ss, sm], axis=1)
    low = jnp.concatenate([sm.T, mm], axis=1)
    return jnp.concatenate([top, low], axis=0)


def kernel(
    n_rows, n_pairs, step,
    obs_ref, est_ref, mask_ref, thr_ref, out_ref,
    x, perm, pay, land, res, gmm_out, gmm_in, v_buf, send,
    rs_s, rs_r, ag_s, ag_r, pm_s, pm_r, pg_s, pg_r, out_s, out_r, own_sem,
):
    me = lax.axis_index("rows")
    group = lax.axis_index("pairs")
    n = n_rows * n_pairs
    bw = x.shape[2]
    rows = x.shape[3]
    chunks = rows // step
    each = send.shape[1]

    barrier = pltpu.get_barrier_semaphore()
    my_k = me * n_pairs + group

    def greet(i, carry):
        k = lax.rem(my_k + i, n)
        pl.semaphore_signal(
            barrier, inc=1, device_id=(k // n_pairs, lax.rem(k, n_pairs)), device_id_type=MESH
        )
        return carry

    lax.fori_loop(1, n, greet, 0)

    for slot in range(4):
        cols = slice(slot * bw, (slot + 1) * bw)
        for c in range(chunks):
            part = slice(c * step, (c + 1) * step)
            filled = jnp.where(mask_ref[part, cols] == 1, obs_ref[part, cols], est_ref[part, cols])
            x[0, slot, :, part] = filled.T

    def cols_of(c):
        return pl.ds(pl.multiple_of(c * step, step), step)

    def full_gram(s, m):
        total = jnp.zeros((2 * bw, 2 * bw), F32)
        for c in range(chunks):
            part = slice(c * step, (c + 1) * step)
            both = split(jnp.concatenate([s[:, part], m[:, part]], axis=0))
            total += dot_parts(both, both, NT)
        return total

    def cross_gram(s, m):
        total = jnp.zeros((bw, bw), F32)
        for c in range(chunks):
            part = slice(c * step, (c + 1) * step)
            total += dot_parts(split(s[:, part]), split(m[:, part]), NT)
        return total

    def all_reduce(b, blocks):
        count = len(blocks)
        piece = count * bw // n_rows
        base = sum(COUNTS[:b]) * bw
        lbase = base // n_rows
        for i, block in enumerate(blocks):
            pay[base + i * bw : base + (i + 1) * bw, :] = block
        if b == 0:
            pl.semaphore_wait(barrier, n - 1)

        def area(ref, p):
            return ref.at[pl.ds(pl.multiple_of(base + p * piece, 8), piece)]

        def scatter(off, carry):
            peer = lax.rem(me + off, n_rows)
            pltpu.make_async_remote_copy(
                area(pay, peer), land.at[off, pl.ds(lbase, piece)],
                rs_s.at[b], rs_r.at[b], device_id=(peer, group), device_id_type=MESH,
            ).start()
            return carry

        lax.fori_loop(1, n_rows, scatter, 0)
        others = land.at[pl.ds(1, n_rows - 1), pl.ds(lbase, piece)]
        pltpu.make_async_copy(others, others, rs_r.at[b]).wait()
        mine = pl.ds(pl.multiple_of(base + me * piece, 8), piece)
        total = pay[mine, :]
        for off in range(1, n_rows):
            total += land[off, lbase : lbase + piece, :]
        res[mine, :] = total

        def gather(off, carry):
            peer = lax.rem(me + off, n_rows)
            pltpu.make_async_remote_copy(
                area(res, me), area(res, me),
                ag_s.at[b], ag_r.at[b], device_id=(peer, group), device_id_type=MESH,
            ).start()
            return carry

        lax.fori_loop(1, n_rows, gather, 0)
        pltpu.make_async_copy(others, others, ag_r.at[b]).wait()
        return [res[base + i * bw : base + (i + 1) * bw, :] for i in range(count)]

    def settle(b):
        piece = COUNTS[b] * bw // n_rows
        lbase = sum(COUNTS[:b]) * bw // n_rows
        others = land.at[pl.ds(1, n_rows - 1), pl.ds(lbase, piece)]
        pltpu.make_async_copy(others, others, rs_s.at[b]).wait()
        pltpu.make_async_copy(others, others, ag_s.at[b]).wait()

    def put(v_half, s, m, write):
        v_parts = split(v_half)
        for c in range(chunks):
            part = slice(c * step, (c + 1) * step)
            both = split(jnp.concatenate([s[:, part], m[:, part]], axis=0))
            write(part, dot_parts(v_parts, both, NN))

    def into(ref):
        def write(part, value):
            ref[:, part] = value
        return write

    def pass_on(i, block, gmm):
        gmm_out[i] = gmm
        right = lax.rem(group + 1, n_pairs)
        data = pltpu.make_async_remote_copy(
            block, perm.at[i], pm_s.at[i], pm_r.at[i],
            device_id=(me, right), device_id_type=MESH,
        )
        data.start()
        small = pltpu.make_async_remote_copy(
            gmm_out.at[i], gmm_in.at[i], pg_s.at[i], pg_r.at[i],
            device_id=(me, right), device_id_type=MESH,
        )
        small.start()
        return data, small

    def new_grams(v, gram):
        vg = dot3(v, gram)
        return dot3(vg[:bw], v[:bw], NT), dot3(vg[bw:], v[bw:], NT)

    def deliver(half):
        count = n // 2

        def go(i, carry):
            k = half * count + lax.rem(my_k + i, count)

            @pl.when(k != my_k)
            def _():
                pltpu.make_async_remote_copy(
                    send.at[k], out_ref.at[my_k], out_s, out_r,
                    device_id=(k // n_pairs, lax.rem(k, n_pairs)), device_id_type=MESH,
                ).start()

            @pl.when(k == my_k)
            def _():
                pltpu.make_async_copy(send.at[k], out_ref.at[my_k], own_sem).start()

            return carry

        lax.fori_loop(0, count, go, 0)

    def finish(half, v, gram, s, m):
        vg = dot3(v, gram)
        squares = jnp.sum(vg * v, axis=1, keepdims=True)
        norm = jnp.sqrt(squares + 1e-06)
        level = thr_ref[2 * half * bw : 2 * (half + 1) * bw, :]
        scaled = (jnp.maximum(norm - level, 0.0) / norm) * v
        per_block = bw // each
        for j in range(2):
            def write(part, value):
                for i in range(per_block):
                    send[(2 * half + j) * per_block + i, :, part] = value[i * each : (i + 1) * each]
            put(scaled[j * bw : (j + 1) * bw], s, m, write)
        deliver(half)

    ga = full_gram(x.at[0, 0], x.at[0, 1])
    gb = full_gram(x.at[0, 2], x.at[0, 3])
    blocks = []
    for g in (ga, gb):
        blocks += [g[:bw, :bw], g[:bw, bw:], g[bw:, bw:]]
    got = all_reduce(0, blocks)
    gb = join(*got[3:])
    vb = whitening_t(gb)
    put(vb[bw:], x.at[0, 2], x.at[0, 3], into(x.at[1, 3]))
    bs, bm = new_grams(vb, gb)
    sent = [pass_on(0, x.at[1, 3], bm)]
    ga = join(*got[:3])
    va = whitening_t(ga)
    put(va[bw:], x.at[0, 0], x.at[0, 1], into(x.at[1, 1]))
    put(vb[:bw], x.at[0, 2], x.at[0, 3], into(x.at[1, 2]))
    as_, am = new_grams(va, ga)

    (sm,) = all_reduce(1, [cross_gram(x.at[1, 2], x.at[1, 1])])
    gb = join(bs, sm, am)
    vb = whitening_t(gb)
    put(vb[bw:], x.at[1, 2], x.at[1, 1], into(x.at[2, 3]))
    bs, bm = new_grams(vb, gb)
    sent.append(pass_on(1, x.at[2, 3], bm))
    put(vb[:bw], x.at[1, 2], x.at[1, 1], into(x.at[2, 2]))
    put(va[:bw], x.at[0, 0], x.at[0, 1], into(x.at[1, 0]))

    for c in sent[0]:
        c.wait_recv()
    (sm,) = all_reduce(2, [cross_gram(x.at[1, 0], perm.at[0])])
    ga = join(as_, sm, gmm_in[0])
    va = whitening_t(ga)
    put(va[bw:], x.at[1, 0], perm.at[0], into(x.at[2, 1]))
    put(va[:bw], x.at[1, 0], perm.at[0], into(x.at[2, 0]))
    as_, am = new_grams(va, ga)

    sm_b = cross_gram(x.at[2, 2], x.at[2, 1])
    for c in sent[1]:
        c.wait_recv()
    sm_b, sm_a = all_reduce(3, [sm_b, cross_gram(x.at[2, 0], perm.at[1])])
    gb = join(bs, sm_b, am)
    vb = whitening_t(gb)
    put(vb[bw:], x.at[2, 2], x.at[2, 1], into(x.at[3, 3]))
    bs, bm = new_grams(vb, gb)
    sent.append(pass_on(2, x.at[3, 3], bm))
    ga = join(as_, sm_a, gmm_in[1])
    va = whitening_t(ga)
    put(va[bw:], x.at[2, 0], perm.at[1], into(x.at[3, 1]))
    put(vb[:bw], x.at[2, 2], x.at[2, 1], into(x.at[3, 2]))
    as_, am = new_grams(va, ga)

    (sm,) = all_reduce(4, [cross_gram(x.at[3, 2], x.at[3, 1])])
    gb = join(bs, sm, am)
    finish(1, whitening_t(gb), gb, x.at[3, 2], x.at[3, 1])
    put(va[:bw], x.at[2, 0], perm.at[1], into(x.at[3, 0]))
    for c in sent[2]:
        c.wait_recv()
    (sm,) = all_reduce(5, [cross_gram(x.at[3, 0], perm.at[2])])
    ga = join(as_, sm, gmm_in[2])
    finish(0, whitening_t(ga), ga, x.at[3, 0], perm.at[2])

    for b in range(len(COUNTS)):
        settle(b)
    for pair in sent:
        for c in pair:
            c.wait_send()
    pltpu.make_async_copy(send.at[0], out_ref.at[my_k], own_sem).wait()
    rest = send.at[pl.ds(0, n - 1)]
    pltpu.make_async_copy(rest, rest, out_s).wait()
    arrived = out_ref.at[pl.ds(0, n - 1)]
    pltpu.make_async_copy(arrived, arrived, out_r).wait()


COUNTS = (6, 1, 1, 2, 1, 1)


def on_device(observed, estimate, mask, threshold):
    n_rows = lax.axis_size("rows")
    n_pairs = lax.axis_size("pairs")
    rows, width = observed.shape
    bw = width // 4
    n = n_rows * n_pairs
    each = width // n
    step = 512 if rows % 512 == 0 else rows
    total = sum(COUNTS) * bw
    vmem = pl.BlockSpec(memory_space=pltpu.VMEM)
    dma = pltpu.SemaphoreType.DMA
    nb = len(COUNTS)
    landed = pl.pallas_call(
        functools.partial(kernel, n_rows, n_pairs, step),
        out_shape=jax.ShapeDtypeStruct((n, each, rows), F32),
        in_specs=[vmem] * 4,
        out_specs=pl.BlockSpec(memory_space=pl.ANY),
        scratch_shapes=[
            pltpu.VMEM((4, 4, bw, rows), F32),
            pltpu.VMEM((3, bw, rows), F32),
            pltpu.VMEM((total, bw), F32),
            pltpu.VMEM((n_rows, total // n_rows, bw), F32),
            pltpu.VMEM((total, bw), F32),
            pltpu.VMEM((3, bw, bw), F32),
            pltpu.VMEM((3, bw, bw), F32),
            pltpu.VMEM((8, bw), F32),
            pltpu.VMEM((n, each, rows), F32),
            dma((nb,)), dma((nb,)), dma((nb,)), dma((nb,)),
            dma((3,)), dma((3,)), dma((3,)), dma((3,)),
            dma, dma, dma,
        ],
        compiler_params=pltpu.CompilerParams(
            collective_id=0, has_side_effects=True, vmem_limit_bytes=60 * 1024 * 1024
        ),
    )(observed, estimate, mask, threshold.reshape(width, 1))
    landed = landed.reshape(n_rows, n_pairs, each, rows).transpose(2, 1, 0, 3)
    return landed.reshape(each * n_pairs, n_rows * rows)


def solution(mesh):
    placed = (P("rows", "pairs"), P("rows", "pairs"), P("rows", "pairs"), P("pairs"))
    return jax.shard_map(
        on_device, mesh=mesh, in_specs=placed, out_specs=P(("rows", "pairs"), None), check_vma=False
    )
```

time: 579 us -> 255 us (0.44); the launches traced: 571 us -> 255 us
  waiting for transfers between devices: 276 us -> 0 us
  Pallas kernels: 0 us -> 246 us
  blocking collectives: 88 us -> 0 us
  local copies, waits for them, and re-layouts: 91.6 us -> 8.7 us
  matrix products: 75.5 us -> 0 us
  other arithmetic: 20.6 us -> 0 us
  between operations: 14 us -> 0.01 us
    pallas_call x0 -> x1, Pallas kernels: none -> 246 us  [on_device(): pl.pallas_call(functools.partial(kernel, n_rows, n_pairs, step), out_shap...]
    psum x4 -> x0, waiting for transfers between devices: 225 us -> none  [on_device(): gram = lax.psum(partial_gram, 'rows')]
    dot_general x40 -> x0, matrix products: 75.5 us -> none  [the longest x4 17.7 us: on_device(): partial_gram = jnp.einsum('rpi,rpj->pij', pairs, pairs, precision=HI)]
    all_to_all x1 -> x0, blocking collectives: 74.3 us -> none  [on_device(): lax.all_to_all(packed, ('rows', 'pairs'), split_axis=0, concat_axis=1, ti...]
    psum x4 -> x0, local copies, waits for them, and re-layouts: 69.3 us -> none  [on_device(): gram = lax.psum(partial_gram, 'rows')]
    ppermute x3 -> x0, waiting for transfers between devices: 50.8 us -> none  [from_behind(): return lax.ppermute(block, axis, route)]
    psum x1 -> x0, blocking collectives: 13.7 us -> none  [on_device(): squares = lax.psum(jnp.sum(filled * filled, axis=0), 'rows')]
    gather x4 -> x0, local copies, waits for them, and re-layouts: 11.9 us -> none  [whitening_of(): dsum = jnp.diagonal(gram, axis1=-2, axis2=-1) + 1e-06]
  transfers between devices with their start and end apart: 7 -> 0, of which waited for: 7 -> 0; matrix products, arithmetic and copies ran while one was open for 0% -> 0% of each run, Pallas kernels for 0% -> 0%
where the time goes in v1:
time: 255 us
  Pallas kernels  246 us (96%)
  local copies, waits for them, and re-layouts  8.7 us (3%)
    pallas_call x1, Pallas kernels, on_device(): pl.pallas_call(functools.partial(kernel, n_rows, n_pairs, step), out_shap...  246 us

profile of v1, /device:TPU:0, one launch (start us, length us, event | category | flops | bytes accessed | tf_op | source)
XLA Modules:
  0.0 255.0 jit_solution(17854866615840170574)
XLA Ops:
  0.0 1.5 copy.6.thr_ref
  1.5 246.3 %shard_map.46 = f32[32,16,1536]{2,1,0:T(8,128)} custom-call(f32[1536,512]{1,0:T(8,128)} %obs_ref.1, f32[1536,512]{1,0:T(8,128)} %est_ref.1, s32[1536,512]{1,0:T(8,128)} %mask_ref.1, f32[512,1]{1,0:T(8,128)} %copy.6.thr_ref), custom_call_target="tpu_custom_call" | custom-call | tf_op jit(solution)/shard_map/pallas_call | solution.py:317
  247.8 3.7 %copy.7 = f32[16,4,8,1536]{3,2,1,0:T(8,128)S(1)} copy(f32[16,4,8,1536]{3,0,1,2:T(8,128)} %bitcast.8) | data formatting | bytes 6291456 | tf_op jit(solution)/shard_map/transpose | solution.py:340
  251.6 3.4 %copy.8 = f32[8,8,8,1536]{3,1,2,0:T(8,128)} copy(f32[8,8,8,1536]{3,2,1,0:T(8,128)S(1)} %bitcast.7) | data formatting | bytes 6291456

commit v2 on v1

--- a/solution.py
+++ b/solution.py
@@ -64,7 +64,7 @@
 def kernel(
     n_rows, n_pairs, step,
     obs_ref, est_ref, mask_ref, thr_ref, out_ref,
-    x, perm, pay, land, res, gmm_out, gmm_in, v_buf, send,
+    x, perm, pay, land, res, gmm_out, gmm_in, send,
     rs_s, rs_r, ag_s, ag_r, pm_s, pm_r, pg_s, pg_r, out_s, out_r, own_sem,
 ):
     me = lax.axis_index("rows")
@@ -217,7 +217,12 @@
         vg = dot3(v, gram)
         squares = jnp.sum(vg * v, axis=1, keepdims=True)
         norm = jnp.sqrt(squares + 1e-06)
-        level = thr_ref[2 * half * bw : 2 * (half + 1) * bw, :]
+        eye = (
+            lax.broadcasted_iota(jnp.int32, gram.shape, 0)
+            == lax.broadcasted_iota(jnp.int32, gram.shape, 1)
+        )
+        level = thr_ref[:, 2 * half * bw : 2 * (half + 1) * bw]
+        level = jnp.sum(jnp.where(eye, level, 0.0), axis=1, keepdims=True)
         scaled = (jnp.maximum(norm - level, 0.0) / norm) * v
         per_block = bw // each
         for j in range(2):
@@ -225,7 +230,6 @@
                 for i in range(per_block):
                     send[(2 * half + j) * per_block + i, :, part] = value[i * each : (i + 1) * each]
             put(scaled[j * bw : (j + 1) * bw], s, m, write)
-        deliver(half)
 
     ga = full_gram(x.at[0, 0], x.at[0, 1])
     gb = full_gram(x.at[0, 2], x.at[0, 3])
@@ -286,6 +290,9 @@
     (sm,) = all_reduce(5, [cross_gram(x.at[3, 0], perm.at[2])])
     ga = join(as_, sm, gmm_in[2])
     finish(0, whitening_t(ga), ga, x.at[3, 0], perm.at[2])
+    far = 1 - my_k // (n // 2)
+    deliver(far)
+    deliver(1 - far)
 
     for b in range(len(COUNTS)):
         settle(b)
@@ -297,6 +304,12 @@
     pltpu.make_async_copy(rest, rest, out_s).wait()
     arrived = out_ref.at[pl.ds(0, n - 1)]
     pltpu.make_async_copy(arrived, arrived, out_r).wait()
+
+
+def interleave(in_ref, out_ref):
+    n_pairs, each, _ = in_ref.shape
+    for i in range(each):
+        out_ref[i * n_pairs : (i + 1) * n_pairs, :] = in_ref[:, i, :]
 
 
 COUNTS = (6, 1, 1, 2, 1, 1)
@@ -327,7 +340,6 @@
             pltpu.VMEM((total, bw), F32),
             pltpu.VMEM((3, bw, bw), F32),
             pltpu.VMEM((3, bw, bw), F32),
-            pltpu.VMEM((8, bw), F32),
             pltpu.VMEM((n, each, rows), F32),
             dma((nb,)), dma((nb,)), dma((nb,)), dma((nb,)),
             dma((3,)), dma((3,)), dma((3,)), dma((3,)),
@@ -336,9 +348,15 @@
         compiler_params=pltpu.CompilerParams(
             collective_id=0, has_side_effects=True, vmem_limit_bytes=60 * 1024 * 1024
         ),
-    )(observed, estimate, mask, threshold.reshape(width, 1))
-    landed = landed.reshape(n_rows, n_pairs, each, rows).transpose(2, 1, 0, 3)
-    return landed.reshape(each * n_pairs, n_rows * rows)
+    )(observed, estimate, mask, threshold.reshape(1, width))
+    landed = landed.reshape(n_rows, n_pairs, each, rows)
+    return pl.pallas_call(
+        interleave,
+        grid=(n_rows,),
+        out_shape=jax.ShapeDtypeStruct((each * n_pairs, n_rows * rows), F32),
+        in_specs=[pl.BlockSpec((None, n_pairs, each, rows), lambda r: (r, 0, 0, 0))],
+        out_specs=pl.BlockSpec((each * n_pairs, rows), lambda r: (0, r)),
+    )(landed)
 
 
 def solution(mesh):

time: 255 us -> 194 us (0.76)
  Pallas kernels: 246 us -> 194 us
  local copies, waits for them, and re-layouts: 8.7 us -> 0 us
    pallas_call x1, Pallas kernels: 246 us -> 188 us  [on_device(): pl.pallas_call(functools.partial(kernel, n_rows, n_pairs, step), out_shap...]
    pallas_call x0 -> x1, Pallas kernels: none -> 6.41 us  [on_device(): pl.pallas_call(interleave, grid=(n_rows,), out_shape=jax.ShapeDtypeStruct...]
    transpose x1 -> x0, local copies, waits for them, and re-layouts: 3.71 us -> none  [on_device(): landed = landed.reshape(n_rows, n_pairs, each, rows).transpose(2, 1, 0, 3)]
    unnamed x1 -> x0, local copies, waits for them, and re-layouts: 3.45 us -> none
where the time goes in v2:
time: 194 us
  Pallas kernels  194 us (100%)
    pallas_call x1, Pallas kernels, on_device(): pl.pallas_call(functools.partial(kernel, n_rows, n_pairs, step), out_shap...  188 us
    pallas_call x1, Pallas kernels, on_device(): pl.pallas_call(interleave, grid=(n_rows,), out_shape=jax.ShapeDtypeStruct...  6.41 us

profile of v2, /device:TPU:0, one launch (start us, length us, event | category | flops | bytes accessed | tf_op | source)
XLA Modules:
  0.0 194.0 jit_solution(110750574075445297)
XLA Ops:
  0.0 187.6 %shard_map.46 = f32[32,16,1536]{2,1,0:T(8,128)} custom-call(f32[1536,512]{1,0:T(8,128)} %obs_ref.1, f32[1536,512]{1,0:T(8,128)} %est_ref.1, s32[1536,512]{1,0:T(8,128)} %mask_ref.1, f32[1,512]{1,0:T(1,128)} %bitcast.3), custom_call_target="tpu_custom_call" | custom-call | tf_op jit(solution)/shard_map/pallas_call | solution.py:330
  187.6 6.4 %shard_map.47 = f32[64,12288]{1,0:T(8,128)} custom-call(f32[8,4,16,1536]{3,2,1,0:T(8,128)} %bitcast.2), custom_call_target="tpu_custom_call" | custom-call | tf_op jit(solution)/shard_map/pallas_call | solution.py:353

commit v3 on v2

--- a/solution.py
+++ b/solution.py
@@ -112,31 +112,40 @@
             total += dot_parts(split(s[:, part]), split(m[:, part]), NT)
         return total
 
-    def all_reduce(b, blocks):
-        count = len(blocks)
-        piece = count * bw // n_rows
+    def place(b):
         base = sum(COUNTS[:b]) * bw
-        lbase = base // n_rows
+        piece = COUNTS[b] * bw // n_rows
+        return base, base // n_rows, piece
+
+    def own(b, p):
+        base, _, piece = place(b)
+        return pl.ds(pl.multiple_of(base + p * piece, 8), piece)
+
+    def others(b):
+        _, lbase, piece = place(b)
+        return land.at[pl.ds(1, n_rows - 1), pl.ds(lbase, piece)]
+
+    def reduce_start(b, blocks):
+        base, lbase, piece = place(b)
         for i, block in enumerate(blocks):
             pay[base + i * bw : base + (i + 1) * bw, :] = block
         if b == 0:
             pl.semaphore_wait(barrier, n - 1)
 
-        def area(ref, p):
-            return ref.at[pl.ds(pl.multiple_of(base + p * piece, 8), piece)]
-
         def scatter(off, carry):
             peer = lax.rem(me + off, n_rows)
             pltpu.make_async_remote_copy(
-                area(pay, peer), land.at[off, pl.ds(lbase, piece)],
+                pay.at[own(b, peer)], land.at[off, pl.ds(lbase, piece)],
                 rs_s.at[b], rs_r.at[b], device_id=(peer, group), device_id_type=MESH,
             ).start()
             return carry
 
         lax.fori_loop(1, n_rows, scatter, 0)
-        others = land.at[pl.ds(1, n_rows - 1), pl.ds(lbase, piece)]
-        pltpu.make_async_copy(others, others, rs_r.at[b]).wait()
-        mine = pl.ds(pl.multiple_of(base + me * piece, 8), piece)
+
+    def reduce_mid(b):
+        _, lbase, piece = place(b)
+        pltpu.make_async_copy(others(b), others(b), rs_r.at[b]).wait()
+        mine = own(b, me)
         total = pay[mine, :]
         for off in range(1, n_rows):
             total += land[off, lbase : lbase + piece, :]
@@ -145,21 +154,21 @@
         def gather(off, carry):
             peer = lax.rem(me + off, n_rows)
             pltpu.make_async_remote_copy(
-                area(res, me), area(res, me),
+                res.at[mine], res.at[mine],
                 ag_s.at[b], ag_r.at[b], device_id=(peer, group), device_id_type=MESH,
             ).start()
             return carry
 
         lax.fori_loop(1, n_rows, gather, 0)
-        pltpu.make_async_copy(others, others, ag_r.at[b]).wait()
-        return [res[base + i * bw : base + (i + 1) * bw, :] for i in range(count)]
+
+    def reduce_end(b):
+        base, _, _ = place(b)
+        pltpu.make_async_copy(others(b), others(b), ag_r.at[b]).wait()
+        return [res[base + i * bw : base + (i + 1) * bw, :] for i in range(COUNTS[b])]
 
     def settle(b):
-        piece = COUNTS[b] * bw // n_rows
-        lbase = sum(COUNTS[:b]) * bw // n_rows
-        others = land.at[pl.ds(1, n_rows - 1), pl.ds(lbase, piece)]
-        pltpu.make_async_copy(others, others, rs_s.at[b]).wait()
-        pltpu.make_async_copy(others, others, ag_s.at[b]).wait()
+        pltpu.make_async_copy(others(b), others(b), rs_s.at[b]).wait()
+        pltpu.make_async_copy(others(b), others(b), ag_s.at[b]).wait()
 
     def put(v_half, s, m, write):
         v_parts = split(v_half)
@@ -173,20 +182,25 @@
             ref[:, part] = value
         return write
 
-    def pass_on(i, block, gmm):
+    right = lax.rem(group + 1, n_pairs)
+
+    def pass_copy(src, dst, send_sem, recv_sem):
+        return pltpu.make_async_remote_copy(
+            src, dst, send_sem, recv_sem, device_id=(me, right), device_id_type=MESH
+        )
+
+    def put_and_pass(i, v_half, s, m, block):
+        def write(part, value):
+            block[:, part] = value
+            pass_copy(block.at[:, part], perm.at[i, :, part], pm_s.at[i], pm_r.at[i]).start()
+
+        put(v_half, s, m, write)
+
+    def pass_gram(i, block, gmm):
         gmm_out[i] = gmm
-        right = lax.rem(group + 1, n_pairs)
-        data = pltpu.make_async_remote_copy(
-            block, perm.at[i], pm_s.at[i], pm_r.at[i],
-            device_id=(me, right), device_id_type=MESH,
-        )
-        data.start()
-        small = pltpu.make_async_remote_copy(
-            gmm_out.at[i], gmm_in.at[i], pg_s.at[i], pg_r.at[i],
-            device_id=(me, right), device_id_type=MESH,
-        )
+        small = pass_copy(gmm_out.at[i], gmm_in.at[i], pg_s.at[i], pg_r.at[i])
         small.start()
-        return data, small
+        return pass_copy(block, perm.at[i], pm_s.at[i], pm_r.at[i]), small
 
     def new_grams(v, gram):
         vg = dot3(v, gram)
@@ -231,68 +245,75 @@
                     send[(2 * half + j) * per_block + i, :, part] = value[i * each : (i + 1) * each]
             put(scaled[j * bw : (j + 1) * bw], s, m, write)
 
-    ga = full_gram(x.at[0, 0], x.at[0, 1])
-    gb = full_gram(x.at[0, 2], x.at[0, 3])
-    blocks = []
-    for g in (ga, gb):
-        blocks += [g[:bw, :bw], g[:bw, bw:], g[bw:, bw:]]
-    got = all_reduce(0, blocks)
-    gb = join(*got[3:])
+    def thirds(g):
+        return [g[:bw, :bw], g[:bw, bw:], g[bw:, bw:]]
+
+    reduce_start(0, thirds(full_gram(x.at[0, 2], x.at[0, 3])))
+    reduce_start(1, thirds(full_gram(x.at[0, 0], x.at[0, 1])))
+    reduce_mid(0)
+    reduce_mid(1)
+    gb = join(*reduce_end(0))
     vb = whitening_t(gb)
-    put(vb[bw:], x.at[0, 2], x.at[0, 3], into(x.at[1, 3]))
+    put_and_pass(0, vb[bw:], x.at[0, 2], x.at[0, 3], x.at[1, 3])
     bs, bm = new_grams(vb, gb)
-    sent = [pass_on(0, x.at[1, 3], bm)]
-    ga = join(*got[:3])
+    sent = [pass_gram(0, x.at[1, 3], bm)]
+    put(vb[:bw], x.at[0, 2], x.at[0, 3], into(x.at[1, 2]))
+    ga = join(*reduce_end(1))
     va = whitening_t(ga)
     put(va[bw:], x.at[0, 0], x.at[0, 1], into(x.at[1, 1]))
-    put(vb[:bw], x.at[0, 2], x.at[0, 3], into(x.at[1, 2]))
+
+    reduce_start(2, [cross_gram(x.at[1, 2], x.at[1, 1])])
+    put(va[:bw], x.at[0, 0], x.at[0, 1], into(x.at[1, 0]))
+    reduce_mid(2)
     as_, am = new_grams(va, ga)
-
-    (sm,) = all_reduce(1, [cross_gram(x.at[1, 2], x.at[1, 1])])
-    gb = join(bs, sm, am)
+    gb = join(bs, *reduce_end(2), am)
     vb = whitening_t(gb)
-    put(vb[bw:], x.at[1, 2], x.at[1, 1], into(x.at[2, 3]))
+    put_and_pass(1, vb[bw:], x.at[1, 2], x.at[1, 1], x.at[2, 3])
     bs, bm = new_grams(vb, gb)
-    sent.append(pass_on(1, x.at[2, 3], bm))
-    put(vb[:bw], x.at[1, 2], x.at[1, 1], into(x.at[2, 2]))
-    put(va[:bw], x.at[0, 0], x.at[0, 1], into(x.at[1, 0]))
+    sent.append(pass_gram(1, x.at[2, 3], bm))
 
     for c in sent[0]:
         c.wait_recv()
-    (sm,) = all_reduce(2, [cross_gram(x.at[1, 0], perm.at[0])])
-    ga = join(as_, sm, gmm_in[0])
+    reduce_start(3, [cross_gram(x.at[1, 0], perm.at[0])])
+    put(vb[:bw], x.at[1, 2], x.at[1, 1], into(x.at[2, 2]))
+    reduce_mid(3)
+    ga = join(as_, *reduce_end(3), gmm_in[0])
     va = whitening_t(ga)
     put(va[bw:], x.at[1, 0], perm.at[0], into(x.at[2, 1]))
+
+    reduce_start(4, [cross_gram(x.at[2, 2], x.at[2, 1])])
     put(va[:bw], x.at[1, 0], perm.at[0], into(x.at[2, 0]))
     as_, am = new_grams(va, ga)
-
-    sm_b = cross_gram(x.at[2, 2], x.at[2, 1])
     for c in sent[1]:
         c.wait_recv()
-    sm_b, sm_a = all_reduce(3, [sm_b, cross_gram(x.at[2, 0], perm.at[1])])
-    gb = join(bs, sm_b, am)
+    reduce_mid(4)
+    reduce_start(5, [cross_gram(x.at[2, 0], perm.at[1])])
+    gb = join(bs, *reduce_end(4), am)
+    reduce_mid(5)
     vb = whitening_t(gb)
-    put(vb[bw:], x.at[2, 2], x.at[2, 1], into(x.at[3, 3]))
+    put_and_pass(2, vb[bw:], x.at[2, 2], x.at[2, 1], x.at[3, 3])
     bs, bm = new_grams(vb, gb)
-    sent.append(pass_on(2, x.at[3, 3], bm))
-    ga = join(as_, sm_a, gmm_in[1])
+    sent.append(pass_gram(2, x.at[3, 3], bm))
+    put(vb[:bw], x.at[2, 2], x.at[2, 1], into(x.at[3, 2]))
+    ga = join(as_, *reduce_end(5), gmm_in[1])
     va = whitening_t(ga)
     put(va[bw:], x.at[2, 0], perm.at[1], into(x.at[3, 1]))
-    put(vb[:bw], x.at[2, 2], x.at[2, 1], into(x.at[3, 2]))
+
+    reduce_start(6, [cross_gram(x.at[3, 2], x.at[3, 1])])
+    put(va[:bw], x.at[2, 0], perm.at[1], into(x.at[3, 0]))
     as_, am = new_grams(va, ga)
-
-    (sm,) = all_reduce(4, [cross_gram(x.at[3, 2], x.at[3, 1])])
-    gb = join(bs, sm, am)
-    finish(1, whitening_t(gb), gb, x.at[3, 2], x.at[3, 1])
-    put(va[:bw], x.at[2, 0], perm.at[1], into(x.at[3, 0]))
+    reduce_mid(6)
+    gb = join(bs, *reduce_end(6), am)
+    vb = whitening_t(gb)
     for c in sent[2]:
         c.wait_recv()
-    (sm,) = all_reduce(5, [cross_gram(x.at[3, 0], perm.at[2])])
-    ga = join(as_, sm, gmm_in[2])
+    reduce_start(7, [cross_gram(x.at[3, 0], perm.at[2])])
+    finish(1, vb, gb, x.at[3, 2], x.at[3, 1])
+    reduce_mid(7)
+    ga = join(as_, *reduce_end(7), gmm_in[2])
+    deliver(1)
     finish(0, whitening_t(ga), ga, x.at[3, 0], perm.at[2])
-    far = 1 - my_k // (n // 2)
-    deliver(far)
-    deliver(1 - far)
+    deliver(0)
 
     for b in range(len(COUNTS)):
         settle(b)
@@ -312,7 +333,7 @@
         out_ref[i * n_pairs : (i + 1) * n_pairs, :] = in_ref[:, i, :]
 
 
-COUNTS = (6, 1, 1, 2, 1, 1)
+COUNTS = (3, 3, 1, 1, 1, 1, 1, 1)
 
 
 def on_device(observed, estimate, mask, threshold):

time: 194 us -> 185 us (0.954)
  Pallas kernels: 194 us -> 185 us
    pallas_call x1, Pallas kernels: 188 us -> 178 us  [on_device(): pl.pallas_call(functools.partial(kernel, n_rows, n_pairs, step), out_shap...]
where the time goes in v3:
time: 185 us
  Pallas kernels  185 us (100%)
    pallas_call x1, Pallas kernels, on_device(): pl.pallas_call(functools.partial(kernel, n_rows, n_pairs, step), out_shap...  178 us
    pallas_call x1, Pallas kernels, on_device(): pl.pallas_call(interleave, grid=(n_rows,), out_shape=jax.ShapeDtypeStruct...  6.41 us

profile of v3, /device:TPU:0, one launch (start us, length us, event | category | flops | bytes accessed | tf_op | source)
XLA Modules:
  0.0 184.7 jit_solution(17124665751607499344)
XLA Ops:
  0.0 178.2 %shard_map.46 = f32[32,16,1536]{2,1,0:T(8,128)} custom-call(f32[1536,512]{1,0:T(8,128)} %obs_ref.1, f32[1536,512]{1,0:T(8,128)} %est_ref.1, s32[1536,512]{1,0:T(8,128)} %mask_ref.1, f32[1,512]{1,0:T(1,128)} %bitcast.3), custom_call_target="tpu_custom_call" | custom-call | tf_op jit(solution)/shard_map/pallas_call | solution.py:351
  178.2 6.4 %shard_map.47 = f32[64,12288]{1,0:T(8,128)} custom-call(f32[8,4,16,1536]{3,2,1,0:T(8,128)} %bitcast.2), custom_call_target="tpu_custom_call" | custom-call | tf_op jit(solution)/shard_map/pallas_call | solution.py:374
